TPU v7x, 256 devices: a whole 4x4x8 slice. The times are simulated.
256 devices in a mesh: row: 16 (over z, core), col: 16 (over y, x).
Axes of the slice: x: 4, y: 4, z: 8, core: 2. Of those that a mesh axis runs over, the one named last changes fastest.
Arguments:
- eigenvectors: float32 [8192, 2048], P('row', 'col'), may hold values from -6 to 6
- aligned_vectors: float32 [2, 8192, 256], P(None, 'row', 'col'), may hold values from -0.3 to 1, as said below
- straddle_vectors: float32 [2, 8192, 256], P(None, 'row', 'col'), may hold values from -0.3 to 1, as said below
Outputs:
- transformed: float32 [8192, 2048], P('row', 'col')
Inputs may be any that keep to these rules, and one draw needn't show every extreme that they name: `aligned_vectors`: within each block of 512 rows, column i is 1 in the block's row i and 0 in the rows above it. `straddle_vectors`: within each straddling block of the steps, column i is 1 in the block's row i and 0 in the rows above it.
All inputs are finite; a program needn't handle non-finite values.
Results may differ from a plain program's by a relative error of at most 0.00027.
Values sent between devices are 32-bit elements; how exact they have to be, the bound alone decides.
A program may use at most 128 MiB of HBM per device.

v0:
```python
import jax
import jax.numpy as jnp
from jax import lax
from jax.experimental import pallas as pl
from jax.experimental.pallas import tpu as pltpu
from jax.sharding import PartitionSpec as P

NB = 256
SPAN = 2 * NB
SIDE = 4
MESH = pl.DeviceIdType.MESH
HIGH = lax.Precision.HIGH


def mm(left, right):
    return lax.dot_general(
        left, right, (((1,), (0,)), ((), ())), precision=HIGH, preferred_element_type=jnp.float32
    )


def mmt(left, right):
    return lax.dot_general(
        left, right, (((1,), (1,)), ((), ())), precision=HIGH, preferred_element_type=jnp.float32
    )


def lower_inverses(grams):
    row = lax.broadcasted_iota(jnp.int32, (NB, NB), 0)
    col = lax.broadcasted_iota(jnp.int32, (NB, NB), 1)
    on_diagonal = row == col
    eye = jnp.where(on_diagonal, 1.0, 0.0)
    small = (row // 32 == col // 32) & (row > col)
    down = [0.5 * jnp.sum(jnp.where(on_diagonal, g, 0.0), axis=1, keepdims=True) for g in grams]
    across = [0.5 * jnp.sum(jnp.where(on_diagonal, g, 0.0), axis=0, keepdims=True) for g in grams]
    powers = [jnp.where(small, g, 0.0) / d for g, d in zip(grams, down)]
    result = [eye - n for n in powers]
    for _ in range(4):
        powers = [mm(n, n) for n in powers]
        result = [t + mm(t, n) for t, n in zip(result, powers)]
    result = [t / d for t, d in zip(result, across)]
    for size in (32, 64, 128):
        below = (row // (2 * size) == col // (2 * size)) & (row // size > col // size)
        left = [mm(t, jnp.where(below, g, 0.0)) for t, g in zip(result, grams)]
        result = [t - mm(half, t) for t, half in zip(result, left)]
    return result


def kernel(
    c_ref, a_ref, x_ref, o_ref,
    A, X, Ct, gram_a, gram_l, gram_u, gram_in, t_a, t_l, t_u, g_t, h_t, b_1, b_2, m_t,
    p_own, p_in, P_own, P_in,
    ring_send, ring_recv, row_send, row_recv,
):
    row = lax.axis_index("row")
    col = lax.axis_index("col")
    last = lax.axis_size("row") - 1
    y, x = col // SIDE, col % SIDE

    def at_x(step):
        return (row, y * SIDE + (x + step + SIDE) % SIDE)

    def at_y(step):
        return (row, ((y + step + SIDE) % SIDE) * SIDE + x)

    above = ((row + last) % (last + 1), col)
    below = ((row + 1) % (last + 1), col)
    has_above = row > 0
    has_below = row < last

    def remote(src, dst, sems, index, device):
        send, recv = sems
        return pltpu.make_async_remote_copy(
            src_ref=src, dst_ref=dst, send_sem=send.at[index], recv_sem=recv.at[index],
            device_id=device, device_id_type=MESH,
        )

    ring = (ring_send, ring_recv)
    rows = (row_send, row_recv)

    barrier = pltpu.get_barrier_semaphore()
    for device in (at_x(1), at_x(-1), at_y(1), at_y(-1)):
        pl.semaphore_signal(barrier, inc=1, device_id=device, device_id_type=MESH)

    @pl.when(has_above)
    def _():
        pl.semaphore_signal(barrier, inc=1, device_id=above, device_id_type=MESH)

    @pl.when(has_below)
    def _():
        pl.semaphore_signal(barrier, inc=1, device_id=below, device_id_type=MESH)

    ends = (row + last) // (last + 1) + (2 * last - row) // (last + 1)
    pl.semaphore_wait(barrier, 4 + ends)

    def a_one(k):
        return A.at[:, y, (x + k + SIDE) % SIDE]

    def a_line(k):
        return A.at[:, (y + k + SIDE) % SIDE]

    def x_one(k):
        return X.at[:, (y + k + SIDE) % SIDE, x]

    def x_line(k):
        return X.at[:, :, (x + k + SIDE) % SIDE]

    def ring_stage(base, own, slot, device):
        right = remote(own, slot(0), ring, base, device(1))
        left = remote(own, slot(0), ring, base + 1, device(-1))
        on_right = remote(slot(-1).at[0], slot(-1).at[0], ring, base + 2, device(1))
        on_left = remote(slot(1).at[1], slot(1).at[1], ring, base + 3, device(-1))
        return right, left, on_right, on_left

    def begin(stage):
        stage[0].start()
        stage[1].start()

    def pass_on(stage):
        stage[0].wait_recv()
        stage[2].start()
        stage[1].wait_recv()
        stage[3].start()

    def finish(stage):
        stage[2].wait_recv()
        stage[3].wait_recv()

    stage_a1 = ring_stage(0, a_ref, a_one, at_x)
    stage_x1 = ring_stage(4, x_ref, x_one, at_y)
    stage_a2 = ring_stage(8, a_line(0), a_line, at_y)
    stage_x2 = ring_stage(12, x_line(0), x_line, at_x)

    begin(stage_x1)
    begin(stage_a1)
    A[:, y, x] = a_ref[...]
    X[:, y, x] = x_ref[...]

    @pl.when(row == last)
    def _():
        gram_in[...] = jnp.zeros_like(gram_in)
        P_in[...] = jnp.zeros_like(P_in)

    @pl.when(row == 0)
    def _():
        p_in[...] = jnp.zeros_like(p_in)

    pass_on(stage_x1)
    pass_on(stage_a1)
    finish(stage_x1)
    begin(stage_x2)
    finish(stage_a1)
    begin(stage_a2)
    Ct[...] = c_ref[...].T
    pass_on(stage_x2)
    pass_on(stage_a2)
    finish(stage_x2)

    def x_up(s):
        return X[s, :, :, :, :NB].reshape(NB, NB)

    def x_low(s):
        return X[s, :, :, :, NB:].reshape(NB, NB)

    def a_up(s):
        return A[s, :, :, :, :NB].reshape(NB, NB)

    def a_low(s):
        return A[s, :, :, :, NB:].reshape(NB, NB)

    def a_all(s):
        return A[s].reshape(NB, SPAN)

    gram_up = [remote(gram_u.at[s], gram_in.at[s], rows, s, above) for s in range(2)]
    t_down = [remote(t_l.at[s], t_u.at[s], rows, 2 + s, below) for s in range(2)]
    p_down = [remote(p_own.at[s], p_in.at[s], rows, 4 + s, below) for s in range(2)]
    P_up = [remote(P_own.at[s], P_in.at[s], rows, 6 + s, above) for s in range(2)]

    for s in range(2):
        gram_u[s] = mmt(x_up(s), x_up(s))

        @pl.when(has_above)
        def _():
            gram_up[s].start()

        gram_l[s] = mmt(x_low(s), x_low(s))

    p_own[0] = mmt(Ct[:, NB:], x_low(0))

    @pl.when(has_below)
    def _():
        p_down[0].start()

    finish(stage_a2)
    for s in range(2):
        gram_a[s] = mmt(a_all(s), a_all(s))
        g_t[s] = mmt(x_low(s), a_low(s))
        h_t[s] = mmt(a_up(s), x_up(s))
    pair = lower_inverses([gram_a[0], gram_a[1]])
    for s in range(2):
        t_a[s] = pair[s]
        b_2[s] = mm(t_a[s], h_t[s])

    @pl.when(has_below)
    def _():
        for s in range(2):
            gram_up[s].wait_recv()

    pair = lower_inverses([gram_l[0] + gram_in[0], gram_l[1] + gram_in[1]])
    for s in range(2):
        t_l[s] = pair[s]

        @pl.when(has_below)
        def _():
            t_down[s].start()

    for s in range(2):
        b_1[s] = mm(t_l[s], g_t[s])
        m_t[s] = mm(b_1[s], b_2[s])

    @pl.when(row == 0)
    def _():
        own = lower_inverses([gram_u[0], gram_u[1]])
        for s in range(2):
            t_u[s] = own[s]

    for s in range(2):
        w = mmt(Ct[...], a_all(s))
        base = mmt(Ct[:, :NB], x_up(s)) - mm(w, b_2[s])

        @pl.when(has_below)
        def _():
            P_up[s].wait_recv()

        both = p_own[s] + P_in[s]
        P_own[s] = base + mm(both, m_t[s])

        @pl.when(has_above)
        def _():
            P_up[s].start()

        coeffs_a = mm(w - mm(both, b_1[s]), t_a[s])
        coeffs_l = mm(both, t_l[s])
        Ct[:, NB:] = Ct[:, NB:] - mm(coeffs_l, x_low(s)) - mm(coeffs_a, a_low(s))
        if s == 0:
            p_own[1] = mmt(Ct[:, NB:], x_low(1))

            @pl.when(has_below)
            def _():
                p_down[1].start()

        @pl.when(has_above)
        def _():
            p_down[s].wait_recv()
            if s == 0:
                for later in range(2):
                    t_down[later].wait_recv()

        coeffs_u = mm(p_in[s] + P_own[s], t_u[s])
        Ct[:, :NB] = Ct[:, :NB] - mm(coeffs_a, a_up(s)) - mm(coeffs_u, x_up(s))

    o_ref[...] = Ct[...].T

    for stage in (stage_a1, stage_x1, stage_a2, stage_x2):
        for copy in stage:
            copy.wait_send()

    @pl.when(has_above)
    def _():
        for copy in gram_up + P_up:
            copy.wait_send()

    @pl.when(has_below)
    def _():
        for copy in t_down + p_down:
            copy.wait_send()


def on_device(eigenvectors, aligned_vectors, straddle_vectors):
    columns = eigenvectors.shape[1]
    whole = pl.BlockSpec(memory_space=pltpu.VMEM)
    square = pltpu.VMEM((2, NB, NB), jnp.float32)
    gathered = pltpu.VMEM((2, SIDE, SIDE, 16, SPAN), jnp.float32)
    product = pltpu.VMEM((2, columns, NB), jnp.float32)
    return pl.pallas_call(
        kernel,
        out_shape=jax.ShapeDtypeStruct(eigenvectors.shape, jnp.float32),
        in_specs=[whole] * 3,
        out_specs=whole,
        scratch_shapes=[gathered, gathered, pltpu.VMEM((columns, SPAN), jnp.float32)]
        + [square] * 12
        + [product] * 4
        + [
            pltpu.SemaphoreType.DMA((16,)),
            pltpu.SemaphoreType.DMA((16,)),
            pltpu.SemaphoreType.DMA((8,)),
            pltpu.SemaphoreType.DMA((8,)),
        ],
        compiler_params=pltpu.CompilerParams(
            collective_id=0, has_side_effects=True, vmem_limit_bytes=48 * 1024 * 1024
        ),
    )(
        eigenvectors,
        jnp.swapaxes(aligned_vectors, 1, 2),
        jnp.swapaxes(straddle_vectors, 1, 2),
    )


def solution(mesh):
    placed = (P("row", "col"), P(None, "row", "col"), P(None, "row", "col"))
    return jax.shard_map(
        on_device, mesh=mesh, in_specs=placed, out_specs=P("row", "col"), check_vma=False
    )
```

profile of v0, /device:TPU:1, one launch (start us, length us, event | category | flops | bytes accessed | tf_op | source)
XLA Modules:
  0.0 89.7 jit_solution(10847551339151108011)
XLA Ops:
  0.0 0.0 copy-start
  0.0 0.9 %copy-done = f32[512,128]{1,0:T(8,128)S(1)} copy-done((f32[512,128]{1,0:T(8,128)S(1)}, f32[512,128]{1,0:T(8,128)}, u32[]{:S(2)}) %copy-start) | copy-done | bytes 262168
  1.0 0.0 copy-start.1
  1.0 0.8 copy-done.1
  1.8 0.0 copy-start.2
  1.8 0.8 copy-done.2
  2.6 86.4 %shard_map.37 = f32[512,128]{1,0:T(8,128)S(1)} custom-call(f32[512,128]{1,0:T(8,128)S(1)} %copy-done, f32[2,16,512]{2,1,0:T(8,128)S(1)} %bitcast.2, f32[2,16,512]{2,1,0:T(8,128)S(1)} %bitcast.3), custom_call_target="tpu_custom_call" | custom-call | tf_op jit(solution)/shard_map/pallas_call | solution.py:284
  89.0 0.7 copy.5
Async XLA Ops:
  0.0 0.9 %copy-start = (f32[512,128]{1,0:T(8,128)S(1)}, f32[512,128]{1,0:T(8,128)}, u32[]{:S(2)}) copy-start(f32[512,128]{1,0:T(8,128)} %c_ref.1) | copy-start | bytes 786436
  1.0 0.8 copy-start.1
  1.8 0.8 copy-start.2
where the time goes:
time: 89.9 us; the launch traced here: 89.7 us
  Pallas kernels  86.4 us (96%)
  local copies, waits for them, and re-layouts  3.33 us (4%)
    pallas_call x1, Pallas kernels, on_device(): pl.pallas_call(kernel, out_shape=jax.ShapeDtypeStruct(eigenvectors.shape,...  86.4 us
    unnamed x7, local copies, waits for them, and re-layouts  3.33 us

commit v1 on v0

v1 whole, which is shorter than its diff:
```python
import jax
import jax.numpy as jnp
from jax import lax
from jax.experimental import pallas as pl
from jax.experimental.pallas import tpu as pltpu
from jax.sharding import PartitionSpec as P

NB = 256
SPAN = 2 * NB
SIDE = 4
PIECES = 4
PIECE = 32
MESH = pl.DeviceIdType.MESH
HIGH = lax.Precision.HIGH


def mm(left, right):
    return lax.dot_general(
        left, right, (((1,), (0,)), ((), ())), precision=HIGH, preferred_element_type=jnp.float32
    )


def mmt(left, right):
    return lax.dot_general(
        left, right, (((1,), (1,)), ((), ())), precision=HIGH, preferred_element_type=jnp.float32
    )


def lower_inverses(grams, between=()):
    between = list(between)

    def pause():
        if between:
            between.pop(0)()

    row = lax.broadcasted_iota(jnp.int32, (NB, NB), 0)
    col = lax.broadcasted_iota(jnp.int32, (NB, NB), 1)
    on_diagonal = row == col
    eye = jnp.where(on_diagonal, 1.0, 0.0)
    small = (row // 32 == col // 32) & (row > col)
    down = [0.5 * jnp.sum(jnp.where(on_diagonal, g, 0.0), axis=1, keepdims=True) for g in grams]
    across = [0.5 * jnp.sum(jnp.where(on_diagonal, g, 0.0), axis=0, keepdims=True) for g in grams]
    powers = [jnp.where(small, g, 0.0) / d for g, d in zip(grams, down)]
    result = [eye - n for n in powers]
    for _ in range(4):
        powers = [mm(n, n) for n in powers]
        result = [t + mm(t, n) for t, n in zip(result, powers)]
    pause()
    result = [t / d for t, d in zip(result, across)]
    for size in (32, 64, 128):
        below = (row // (2 * size) == col // (2 * size)) & (row // size > col // size)
        left = [mm(t, jnp.where(below, g, 0.0)) for t, g in zip(result, grams)]
        result = [t - mm(half, t) for t, half in zip(result, left)]
        pause()
    return result


def kernel(
    c_ref, a_ref, x_ref, o_ref,
    V, C_in, Ct, gram_a, gram_l, gram_u, gram_in, t_a, t_l, t_u, g_t, h_t, b_1, b_2, m_t,
    p_own, p_in, P_own, P_in,
    ring_send, ring_recv, row_send, row_recv, chain_send, chain_recv, local_sem,
):
    row = lax.axis_index("row")
    col = lax.axis_index("col")
    last = lax.axis_size("row") - 1
    y, x = col // SIDE, col % SIDE

    def at_x(step):
        return (row, y * SIDE + (x + step + SIDE) % SIDE)

    def at_y(step):
        return (row, ((y + step + SIDE) % SIDE) * SIDE + x)

    above = ((row + last) % (last + 1), col)
    below = ((row + 1) % (last + 1), col)
    has_above = row > 0
    has_below = row < last

    def remote(src, dst, sems, index, device):
        send, recv = sems
        return pltpu.make_async_remote_copy(
            src_ref=src, dst_ref=dst, send_sem=send.at[index], recv_sem=recv.at[index],
            device_id=device, device_id_type=MESH,
        )

    ring = (ring_send, ring_recv)
    rows = (row_send, row_recv)
    chain = (chain_send, chain_recv)

    barrier = pltpu.get_barrier_semaphore()
    for device in (at_x(1), at_x(-1), at_y(1), at_y(-1)):
        pl.semaphore_signal(barrier, inc=1, device_id=device, device_id_type=MESH)

    @pl.when(has_above)
    def _():
        pl.semaphore_signal(barrier, inc=1, device_id=above, device_id_type=MESH)

    @pl.when(has_below)
    def _():
        pl.semaphore_signal(barrier, inc=1, device_id=below, device_id_type=MESH)

    def own_block(group, half):
        source = x_ref if group % 2 == 0 else a_ref
        return source.at[group // 2, :, pl.ds((1 - half) * NB, NB)]

    def one(group, half, k):
        if half == 0:
            return V.at[group, half, y, (x + k + SIDE) % SIDE]
        return V.at[group, half, (y + k + SIDE) % SIDE, x]

    def line(group, half, k):
        if half == 0:
            return V.at[group, half, (y + k + SIDE) % SIDE]
        return V.at[group, half, :, (x + k + SIDE) % SIDE]

    own_copies = [
        pltpu.make_async_copy(own_block(g, h), one(g, h, 0), local_sem.at[2 * g + h])
        for g in range(4) for h in range(2)
    ]
    c_copy = pltpu.make_async_copy(c_ref, C_in, local_sem.at[8])
    for copy in own_copies:
        copy.start()
    c_copy.start()

    def ring_stage(base, own, slot, device, split):
        first, second = pl.ds(0, split), pl.ds(split, split)
        return (
            remote(own, slot(0), ring, base, device(1)),
            remote(own, slot(0), ring, base + 1, device(-1)),
            remote(slot(-1).at[first], slot(-1).at[first], ring, base + 2, device(1)),
            remote(slot(1).at[second], slot(1).at[second], ring, base + 3, device(-1)),
        )

    def begin(stage):
        stage[0].start()
        stage[1].start()

    def pass_on(stage):
        stage[0].wait_recv()
        stage[2].start()
        stage[1].wait_recv()
        stage[3].start()

    def finish(stage):
        stage[2].wait_recv()
        stage[3].wait_recv()

    near, far = {}, {}
    for g in range(4):
        for h in range(2):
            base = 8 * (2 * g + h)
            axes = (at_x, at_y) if h == 0 else (at_y, at_x)
            near[g, h] = ring_stage(
                base, own_block(g, h), lambda k, g=g, h=h: one(g, h, k), axes[0], 8
            )
            far[g, h] = ring_stage(
                base + 4, line(g, h, 0), lambda k, g=g, h=h: line(g, h, k), axes[1], 2
            )

    def near_to_far(g):
        for h in range(2):
            finish(near[g, h])
            begin(far[g, h])

    def far_pass(g):
        for h in range(2):
            pass_on(far[g, h])

    def far_finish(g):
        for h in range(2):
            finish(far[g, h])

    ends = (row + last) // (last + 1) + (2 * last - row) // (last + 1)
    pl.semaphore_wait(barrier, 4 + ends)
    for g in range(4):
        for h in range(2):
            begin(near[g, h])

    @pl.when(row == last)
    def _():
        gram_in[...] = jnp.zeros_like(gram_in)
        P_in[...] = jnp.zeros_like(P_in)

    @pl.when(row == 0)
    def _():
        p_in[...] = jnp.zeros_like(p_in)

    for copy in own_copies:
        copy.wait()
    for g in range(4):
        for h in range(2):
            pass_on(near[g, h])
    near_to_far(0)
    near_to_far(1)
    c_copy.wait()
    Ct[...] = C_in[...].T
    far_pass(0)
    near_to_far(2)
    far_pass(1)
    near_to_far(3)

    def x_up(s):
        return V[2 * s, 1].reshape(NB, NB)

    def x_low(s):
        return V[2 * s, 0].reshape(NB, NB)

    def a_up(s):
        return V[2 * s + 1, 1].reshape(NB, NB)

    def a_low(s):
        return V[2 * s + 1, 0].reshape(NB, NB)

    gram_up = [remote(gram_u.at[s], gram_in.at[s], rows, s, above) for s in range(2)]
    t_down = [remote(t_l.at[s], t_u.at[s], rows, 2 + s, below) for s in range(2)]
    p_down = [remote(p_own.at[s], p_in.at[s], rows, 4 + s, below) for s in range(2)]
    P_up = [
        [
            remote(
                P_own.at[s, pl.ds(k * PIECE, PIECE)], P_in.at[s, pl.ds(k * PIECE, PIECE)],
                chain, s * PIECES + k, above,
            )
            for k in range(PIECES)
        ]
        for s in range(2)
    ]

    def upper_gram(s):
        gram_u[s] = mmt(x_up(s), x_up(s))

        @pl.when(has_above)
        def _():
            gram_up[s].start()

    def aligned_products(s):
        gram_a[s] = mmt(a_up(s), a_up(s)) + mmt(a_low(s), a_low(s))

    def cross_products(s):
        g_t[s] = mmt(x_low(s), a_low(s))
        h_t[s] = mmt(a_up(s), x_up(s))

    far_finish(0)
    upper_gram(0)
    gram_l[0] = mmt(x_low(0), x_low(0))
    p_own[0] = mmt(Ct[:, NB:], x_low(0))

    @pl.when(has_below)
    def _():
        p_down[0].start()

    far_finish(1)
    aligned_products(0)
    far_pass(2)

    def third_ready():
        far_finish(2)
        upper_gram(1)

    def last_ready():
        far_pass(3)

    t_a[0] = lower_inverses([gram_a[0]], (last_ready, third_ready))[0]
    cross_products(0)
    b_2[0] = mm(t_a[0], h_t[0])
    gram_l[1] = mmt(x_low(1), x_low(1))
    far_finish(3)
    aligned_products(1)
    cross_products(1)

    @pl.when(has_below)
    def _():
        for s in range(2):
            gram_up[s].wait_recv()

    three = lower_inverses([gram_l[0] + gram_in[0], gram_l[1] + gram_in[1], gram_a[1]])
    for s in range(2):
        t_l[s] = three[s]

        @pl.when(has_below)
        def _():
            t_down[s].start()

    t_a[1] = three[2]
    b_2[1] = mm(t_a[1], h_t[1])
    for s in range(2):
        b_1[s] = mm(t_l[s], g_t[s])
        m_t[s] = mm(b_1[s], b_2[s])

    @pl.when(row == 0)
    def _():
        own = lower_inverses([gram_u[0], gram_u[1]])
        for s in range(2):
            t_u[s] = own[s]

    for s in range(2):
        upper, lower = Ct[:, :NB], Ct[:, NB:]
        w = mmt(upper, a_up(s)) + mmt(lower, a_low(s))
        P_own[s] = mmt(upper, x_up(s)) - mm(w, b_2[s]) + mm(p_own[s], m_t[s])
        for k in range(PIECES):
            piece = pl.ds(k * PIECE, PIECE)

            @pl.when(has_below)
            def _():
                P_up[s][k].wait_recv()
                P_own[s, piece] += mm(P_in[s, piece], m_t[s])

            @pl.when(has_above)
            def _():
                P_up[s][k].start()

        both = p_own[s] + P_in[s]
        coeffs_a = mm(w - mm(both, b_1[s]), t_a[s])
        coeffs_l = mm(both, t_l[s])
        Ct[:, NB:] = lower - mm(coeffs_l, x_low(s)) - mm(coeffs_a, a_low(s))
        if s == 0:
            p_own[1] = mmt(Ct[:, NB:], x_low(1))

            @pl.when(has_below)
            def _():
                p_down[1].start()

        @pl.when(has_above)
        def _():
            p_down[s].wait_recv()
            if s == 0:
                for later in range(2):
                    t_down[later].wait_recv()

        coeffs_u = mm(p_in[s] + P_own[s], t_u[s])
        Ct[:, :NB] = upper - mm(coeffs_a, a_up(s)) - mm(coeffs_u, x_up(s))

    o_ref[...] = Ct[...].T

    for stages in (near, far):
        for stage in stages.values():
            for copy in stage:
                copy.wait_send()

    @pl.when(has_above)
    def _():
        for copy in gram_up + P_up[0] + P_up[1]:
            copy.wait_send()

    @pl.when(has_below)
    def _():
        for copy in t_down + p_down:
            copy.wait_send()


def on_device(eigenvectors, aligned_vectors, straddle_vectors):
    columns = eigenvectors.shape[1]
    in_place = pl.BlockSpec(memory_space=pl.ANY)
    square = pltpu.VMEM((2, NB, NB), jnp.float32)
    product = pltpu.VMEM((2, columns, NB), jnp.float32)
    dma = pltpu.SemaphoreType.DMA
    return pl.pallas_call(
        kernel,
        out_shape=jax.ShapeDtypeStruct(eigenvectors.shape, jnp.float32),
        in_specs=[in_place] * 3,
        out_specs=pl.BlockSpec(memory_space=pltpu.VMEM),
        scratch_shapes=[
            pltpu.VMEM((4, 2, SIDE, SIDE, NB // SIDE**2, NB), jnp.float32),
            pltpu.VMEM(eigenvectors.shape, jnp.float32),
            pltpu.VMEM((columns, SPAN), jnp.float32),
        ]
        + [square] * 12
        + [product] * 4
        + [dma((64,)), dma((64,)), dma((6,)), dma((6,)), dma((2 * PIECES,)), dma((2 * PIECES,)), dma((9,))],
        compiler_params=pltpu.CompilerParams(
            collective_id=0, has_side_effects=True, vmem_limit_bytes=56 * 1024 * 1024
        ),
    )(
        eigenvectors,
        jnp.swapaxes(aligned_vectors, 1, 2),
        jnp.swapaxes(straddle_vectors, 1, 2),
    )


def solution(mesh):
    placed = (P("row", "col"), P(None, "row", "col"), P(None, "row", "col"))
    return jax.shard_map(
        on_device, mesh=mesh, in_specs=placed, out_specs=P("row", "col"), check_vma=False
    )
```

time: 89.9 us -> 82.5 us (0.918)
  Pallas kernels: 86.4 us -> 80.7 us
  local copies, waits for them, and re-layouts: 3.33 us -> 1.67 us
    pallas_call x1, Pallas kernels: 86.4 us -> 80.7 us  [on_device(): pl.pallas_call(kernel, out_shape=jax.ShapeDtypeStruct(eigenvectors.shape,...]
    unnamed x7 -> x1, local copies, waits for them, and re-layouts: 3.33 us -> 1.67 us
where the time goes in v1:
time: 82.5 us; the launch traced here: 82.4 us
  Pallas kernels  80.7 us (98%)
  local copies, waits for them, and re-layouts  1.67 us (2%)
    pallas_call x1, Pallas kernels, on_device(): pl.pallas_call(kernel, out_shape=jax.ShapeDtypeStruct(eigenvectors.shape,...  80.7 us
    unnamed x1, local copies, waits for them, and re-layouts  1.67 us

profile of v1, /device:TPU:1, one launch (start us, length us, event | category | flops | bytes accessed | tf_op | source)
XLA Modules:
  0.0 82.4 jit_solution(12333907142058486601)
XLA Ops:
  0.0 80.7 %shard_map.37 = f32[512,128]{1,0:T(8,128)} custom-call(f32[512,128]{1,0:T(8,128)} %c_ref.1, f32[2,16,512]{2,1,0:T(8,128)} %bitcast.2, f32[2,16,512]{2,1,0:T(8,128)} %bitcast.3), custom_call_target="tpu_custom_call" | custom-call | tf_op jit(solution)/shard_map/pallas_call | solution.py:357
  80.7 1.7 %copy.5 = f32[512,128]{1,0:T(8,128)} copy(f32[512,128]{1,0:T(8,128)} %shard_map.37) | data formatting | bytes 524288

commit v2 on v1

--- a/solution.py
+++ b/solution.py
@@ -7,6 +7,7 @@
 
 NB = 256
 SPAN = 2 * NB
+HALF = NB // 2
 SIDE = 4
 PIECES = 4
 PIECE = 32
@@ -89,7 +90,7 @@
     chain = (chain_send, chain_recv)
 
     barrier = pltpu.get_barrier_semaphore()
-    for device in (at_x(1), at_x(-1), at_y(1), at_y(-1)):
+    for device in (at_x(1), at_x(2), at_x(3), at_y(1), at_y(2), at_y(3)):
         pl.semaphore_signal(barrier, inc=1, device_id=device, device_id_type=MESH)
 
     @pl.when(has_above)
@@ -101,8 +102,8 @@
         pl.semaphore_signal(barrier, inc=1, device_id=below, device_id_type=MESH)
 
     def own_block(group, half):
-        source = x_ref if group % 2 == 0 else a_ref
-        return source.at[group // 2, :, pl.ds((1 - half) * NB, NB)]
+        source = x_ref if group < 2 else a_ref
+        return source.at[group % 2, :, pl.ds((1 - half) * NB, NB)]
 
     def one(group, half, k):
         if half == 0:
@@ -151,16 +152,18 @@
         for h in range(2):
             base = 8 * (2 * g + h)
             axes = (at_x, at_y) if h == 0 else (at_y, at_x)
-            near[g, h] = ring_stage(
-                base, own_block(g, h), lambda k, g=g, h=h: one(g, h, k), axes[0], 8
-            )
+            near[g, h] = [
+                remote(own_block(g, h), one(g, h, 0), ring, base + i, axes[0](k))
+                for i, k in enumerate((1, -1, 2))
+            ]
             far[g, h] = ring_stage(
                 base + 4, line(g, h, 0), lambda k, g=g, h=h: line(g, h, k), axes[1], 2
             )
 
     def near_to_far(g):
         for h in range(2):
-            finish(near[g, h])
+            for copy in near[g, h]:
+                copy.wait_recv()
             begin(far[g, h])
 
     def far_pass(g):
@@ -172,14 +175,21 @@
             finish(far[g, h])
 
     ends = (row + last) // (last + 1) + (2 * last - row) // (last + 1)
-    pl.semaphore_wait(barrier, 4 + ends)
+    pl.semaphore_wait(barrier, 6 + ends)
     for g in range(4):
         for h in range(2):
-            begin(near[g, h])
+            for copy in near[g, h]:
+                copy.start()
+
+    for s in range(2):
+        gram_in[s, :HALF, HALF:] = jnp.zeros((HALF, HALF), jnp.float32)
+        t_u[s, :HALF, HALF:] = jnp.zeros((HALF, HALF), jnp.float32)
 
     @pl.when(row == last)
     def _():
-        gram_in[...] = jnp.zeros_like(gram_in)
+        for s in range(2):
+            gram_in[s, HALF:] = jnp.zeros((HALF, NB), jnp.float32)
+            gram_in[s, :HALF, :HALF] = jnp.zeros((HALF, HALF), jnp.float32)
         P_in[...] = jnp.zeros_like(P_in)
 
     @pl.when(row == 0)
@@ -188,9 +198,6 @@
 
     for copy in own_copies:
         copy.wait()
-    for g in range(4):
-        for h in range(2):
-            pass_on(near[g, h])
     near_to_far(0)
     near_to_far(1)
     c_copy.wait()
@@ -201,20 +208,31 @@
     near_to_far(3)
 
     def x_up(s):
-        return V[2 * s, 1].reshape(NB, NB)
+        return V[s, 1].reshape(NB, NB)
 
     def x_low(s):
-        return V[2 * s, 0].reshape(NB, NB)
+        return V[s, 0].reshape(NB, NB)
 
     def a_up(s):
-        return V[2 * s + 1, 1].reshape(NB, NB)
+        return V[2 + s, 1].reshape(NB, NB)
 
     def a_low(s):
-        return V[2 * s + 1, 0].reshape(NB, NB)
-
-    gram_up = [remote(gram_u.at[s], gram_in.at[s], rows, s, above) for s in range(2)]
-    t_down = [remote(t_l.at[s], t_u.at[s], rows, 2 + s, below) for s in range(2)]
-    p_down = [remote(p_own.at[s], p_in.at[s], rows, 4 + s, below) for s in range(2)]
+        return V[2 + s, 0].reshape(NB, NB)
+
+    def triangle(source, target, s, base, device):
+        return [
+            remote(
+                source.at[s, pl.ds(0, HALF), pl.ds(0, HALF)], target.at[s, pl.ds(0, HALF), pl.ds(0, HALF)],
+                rows, base, device,
+            ),
+            remote(
+                source.at[s, pl.ds(HALF, HALF)], target.at[s, pl.ds(HALF, HALF)], rows, base + 1, device
+            ),
+        ]
+
+    gram_up = [triangle(gram_u, gram_in, s, 2 * s, above) for s in range(2)]
+    t_down = [triangle(t_l, t_u, s, 4 + 2 * s, below) for s in range(2)]
+    p_down = [remote(p_own.at[s], p_in.at[s], rows, 8 + s, below) for s in range(2)]
     P_up = [
         [
             remote(
@@ -231,7 +249,8 @@
 
         @pl.when(has_above)
         def _():
-            gram_up[s].start()
+            for copy in gram_up[s]:
+                copy.start()
 
     def aligned_products(s):
         gram_a[s] = mmt(a_up(s), a_up(s)) + mmt(a_low(s), a_low(s))
@@ -242,28 +261,23 @@
 
     far_finish(0)
     upper_gram(0)
-    gram_l[0] = mmt(x_low(0), x_low(0))
+    far_finish(1)
+    upper_gram(1)
+    for s in range(2):
+        gram_l[s] = mmt(x_low(s), x_low(s))
     p_own[0] = mmt(Ct[:, NB:], x_low(0))
 
     @pl.when(has_below)
     def _():
         p_down[0].start()
 
-    far_finish(1)
+    far_pass(2)
+    far_pass(3)
+    far_finish(2)
     aligned_products(0)
-    far_pass(2)
-
-    def third_ready():
-        far_finish(2)
-        upper_gram(1)
-
-    def last_ready():
-        far_pass(3)
-
-    t_a[0] = lower_inverses([gram_a[0]], (last_ready, third_ready))[0]
+    t_a[0] = lower_inverses([gram_a[0]])[0]
     cross_products(0)
     b_2[0] = mm(t_a[0], h_t[0])
-    gram_l[1] = mmt(x_low(1), x_low(1))
     far_finish(3)
     aligned_products(1)
     cross_products(1)
@@ -271,7 +285,8 @@
     @pl.when(has_below)
     def _():
         for s in range(2):
-            gram_up[s].wait_recv()
+            for copy in gram_up[s]:
+                copy.wait_recv()
 
     three = lower_inverses([gram_l[0] + gram_in[0], gram_l[1] + gram_in[1], gram_a[1]])
     for s in range(2):
@@ -279,7 +294,8 @@
 
         @pl.when(has_below)
         def _():
-            t_down[s].start()
+            for copy in t_down[s]:
+                copy.start()
 
     t_a[1] = three[2]
     b_2[1] = mm(t_a[1], h_t[1])
@@ -323,9 +339,8 @@
         @pl.when(has_above)
         def _():
             p_down[s].wait_recv()
-            if s == 0:
-                for later in range(2):
-                    t_down[later].wait_recv()
+            for copy in t_down[s]:
+                copy.wait_recv()
 
         coeffs_u = mm(p_in[s] + P_own[s], t_u[s])
         Ct[:, :NB] = upper - mm(coeffs_a, a_up(s)) - mm(coeffs_u, x_up(s))
@@ -339,12 +354,12 @@
 
     @pl.when(has_above)
     def _():
-        for copy in gram_up + P_up[0] + P_up[1]:
+        for copy in gram_up[0] + gram_up[1] + P_up[0] + P_up[1]:
             copy.wait_send()
 
     @pl.when(has_below)
     def _():
-        for copy in t_down + p_down:
+        for copy in t_down[0] + t_down[1] + p_down:
             copy.wait_send()
 
 
@@ -366,7 +381,7 @@
         ]
         + [square] * 12
         + [product] * 4
-        + [dma((64,)), dma((64,)), dma((6,)), dma((6,)), dma((2 * PIECES,)), dma((2 * PIECES,)), dma((9,))],
+        + [dma((64,)), dma((64,)), dma((10,)), dma((10,)), dma((2 * PIECES,)), dma((2 * PIECES,)), dma((9,))],
         compiler_params=pltpu.CompilerParams(
             collective_id=0, has_side_effects=True, vmem_limit_bytes=56 * 1024 * 1024
         ),

time: 82.5 us -> 74.7 us (0.905)
  Pallas kernels: 80.7 us -> 72.9 us
    pallas_call x1, Pallas kernels: 80.7 us -> 72.9 us  [on_device(): pl.pallas_call(kernel, out_shape=jax.ShapeDtypeStruct(eigenvectors.shape,...]
where the time goes in v2:
time: 74.7 us; the launch traced here: 74.6 us
  Pallas kernels  72.9 us (98%)
  local copies, waits for them, and re-layouts  1.67 us (2%)
    pallas_call x1, Pallas kernels, on_device(): pl.pallas_call(kernel, out_shape=jax.ShapeDtypeStruct(eigenvectors.shape,...  72.9 us
    unnamed x1, local copies, waits for them, and re-layouts  1.67 us

profile of v2, /device:TPU:1, one launch (start us, length us, event | category | flops | bytes accessed | tf_op | source)
XLA Modules:
  0.0 74.6 jit_solution(5970014407826546016)
XLA Ops:
  0.0 72.9 %shard_map.37 = f32[512,128]{1,0:T(8,128)} custom-call(f32[512,128]{1,0:T(8,128)} %c_ref.1, f32[2,16,512]{2,1,0:T(8,128)} %bitcast.2, f32[2,16,512]{2,1,0:T(8,128)} %bitcast.3), custom_call_target="tpu_custom_call" | custom-call | tf_op jit(solution)/shard_map/pallas_call | solution.py:372
  72.9 1.7 %copy.5 = f32[512,128]{1,0:T(8,128)} copy(f32[512,128]{1,0:T(8,128)} %shard_map.37) | data formatting | bytes 524288

commit v3 on v2

--- a/solution.py
+++ b/solution.py
@@ -58,7 +58,7 @@
 
 def kernel(
     c_ref, a_ref, x_ref, o_ref,
-    V, C_in, Ct, gram_a, gram_l, gram_u, gram_in, t_a, t_l, t_u, g_t, h_t, b_1, b_2, m_t,
+    V, C_in, Ct, gram_a, gram_l, gram_u, gram_in, gram_low, t_a, t_l, t_u, g_t, b_1, b_2, m_t,
     p_own, p_in, P_own, P_in,
     ring_send, ring_recv, row_send, row_recv, chain_send, chain_recv, local_sem,
 ):
@@ -75,6 +75,7 @@
 
     above = ((row + last) % (last + 1), col)
     below = ((row + 1) % (last + 1), col)
+    second = last - 1
     has_above = row > 0
     has_below = row < last
 
@@ -102,7 +103,7 @@
         pl.semaphore_signal(barrier, inc=1, device_id=below, device_id_type=MESH)
 
     def own_block(group, half):
-        source = x_ref if group < 2 else a_ref
+        source = a_ref if group < 2 else x_ref
         return source.at[group % 2, :, pl.ds((1 - half) * NB, NB)]
 
     def one(group, half, k):
@@ -181,6 +182,7 @@
             for copy in near[g, h]:
                 copy.start()
 
+    gram_low[0, :HALF, HALF:] = jnp.zeros((HALF, HALF), jnp.float32)
     for s in range(2):
         gram_in[s, :HALF, HALF:] = jnp.zeros((HALF, HALF), jnp.float32)
         t_u[s, :HALF, HALF:] = jnp.zeros((HALF, HALF), jnp.float32)
@@ -208,16 +210,16 @@
     near_to_far(3)
 
     def x_up(s):
+        return V[2 + s, 1].reshape(NB, NB)
+
+    def x_low(s):
+        return V[2 + s, 0].reshape(NB, NB)
+
+    def a_up(s):
         return V[s, 1].reshape(NB, NB)
 
-    def x_low(s):
+    def a_low(s):
         return V[s, 0].reshape(NB, NB)
-
-    def a_up(s):
-        return V[2 + s, 1].reshape(NB, NB)
-
-    def a_low(s):
-        return V[2 + s, 0].reshape(NB, NB)
 
     def triangle(source, target, s, base, device):
         return [
@@ -244,6 +246,8 @@
         for s in range(2)
     ]
 
+    low_down = triangle(gram_l, gram_low, 0, 10, below)
+
     def upper_gram(s):
         gram_u[s] = mmt(x_up(s), x_up(s))
 
@@ -252,35 +256,40 @@
             for copy in gram_up[s]:
                 copy.start()
 
-    def aligned_products(s):
+    def lower_gram(s):
+        gram_l[s] = mmt(x_low(s), x_low(s))
+
+    def first_x():
+        far_finish(2)
+        lower_gram(0)
+
+        @pl.when(row == second - 1)
+        def _():
+            for copy in low_down:
+                copy.start()
+
+        upper_gram(0)
+
+    for s in range(2):
+        far_finish(s)
         gram_a[s] = mmt(a_up(s), a_up(s)) + mmt(a_low(s), a_low(s))
-
-    def cross_products(s):
+        if s == 0:
+            far_pass(2)
+    pair = lower_inverses([gram_a[0], gram_a[1]], (lambda: far_pass(3), first_x))
+    for s in range(2):
+        t_a[s] = pair[s]
+    p_own[0] = mmt(Ct[:, NB:], x_low(0))
+
+    @pl.when(has_below)
+    def _():
+        p_down[0].start()
+
+    far_finish(3)
+    upper_gram(1)
+    lower_gram(1)
+    for s in range(2):
         g_t[s] = mmt(x_low(s), a_low(s))
-        h_t[s] = mmt(a_up(s), x_up(s))
-
-    far_finish(0)
-    upper_gram(0)
-    far_finish(1)
-    upper_gram(1)
-    for s in range(2):
-        gram_l[s] = mmt(x_low(s), x_low(s))
-    p_own[0] = mmt(Ct[:, NB:], x_low(0))
-
-    @pl.when(has_below)
-    def _():
-        p_down[0].start()
-
-    far_pass(2)
-    far_pass(3)
-    far_finish(2)
-    aligned_products(0)
-    t_a[0] = lower_inverses([gram_a[0]])[0]
-    cross_products(0)
-    b_2[0] = mm(t_a[0], h_t[0])
-    far_finish(3)
-    aligned_products(1)
-    cross_products(1)
+        b_2[s] = mm(t_a[s], mmt(a_up(s), x_up(s)))
 
     @pl.when(has_below)
     def _():
@@ -288,17 +297,37 @@
             for copy in gram_up[s]:
                 copy.wait_recv()
 
-    three = lower_inverses([gram_l[0] + gram_in[0], gram_l[1] + gram_in[1], gram_a[1]])
-    for s in range(2):
-        t_l[s] = three[s]
-
-        @pl.when(has_below)
-        def _():
-            for copy in t_down[s]:
-                copy.start()
-
-    t_a[1] = three[2]
-    b_2[1] = mm(t_a[1], h_t[1])
+
+    @pl.when(row == second)
+    def _():
+        for copy in low_down:
+            copy.wait_recv()
+        three = lower_inverses(
+            [gram_l[0] + gram_in[0], gram_l[1] + gram_in[1], gram_u[0] + gram_low[0]]
+        )
+        t_l[0] = three[0]
+        t_l[1] = three[1]
+        t_u[0] = three[2]
+
+    @pl.when(row != second)
+    def _():
+        two = lower_inverses([gram_l[0] + gram_in[0], gram_l[1] + gram_in[1]])
+        t_l[0] = two[0]
+        t_l[1] = two[1]
+
+    sends_first = has_below & (row != second - 1)
+    takes_first = has_above & (row != second)
+
+    @pl.when(sends_first)
+    def _():
+        for copy in t_down[0]:
+            copy.start()
+
+    @pl.when(has_below)
+    def _():
+        for copy in t_down[1]:
+            copy.start()
+
     for s in range(2):
         b_1[s] = mm(t_l[s], g_t[s])
         m_t[s] = mm(b_1[s], b_2[s])
@@ -339,6 +368,9 @@
         @pl.when(has_above)
         def _():
             p_down[s].wait_recv()
+
+        @pl.when(takes_first if s == 0 else has_above)
+        def _():
             for copy in t_down[s]:
                 copy.wait_recv()
 
@@ -359,13 +391,23 @@
 
     @pl.when(has_below)
     def _():
-        for copy in t_down[0] + t_down[1] + p_down:
+        for copy in t_down[1] + p_down:
+            copy.wait_send()
+
+    @pl.when(sends_first)
+    def _():
+        for copy in t_down[0]:
+            copy.wait_send()
+
+    @pl.when(row == second - 1)
+    def _():
+        for copy in low_down:
             copy.wait_send()
 
 
 def on_device(eigenvectors, aligned_vectors, straddle_vectors):
     columns = eigenvectors.shape[1]
-    in_place = pl.BlockSpec(memory_space=pl.ANY)
+    in_place = pl.BlockSpec(memory_space=pltpu.HBM)
     square = pltpu.VMEM((2, NB, NB), jnp.float32)
     product = pltpu.VMEM((2, columns, NB), jnp.float32)
     dma = pltpu.SemaphoreType.DMA
@@ -381,14 +423,14 @@
         ]
         + [square] * 12
         + [product] * 4
-        + [dma((64,)), dma((64,)), dma((10,)), dma((10,)), dma((2 * PIECES,)), dma((2 * PIECES,)), dma((9,))],
+        + [dma((64,)), dma((64,)), dma((12,)), dma((12,)), dma((2 * PIECES,)), dma((2 * PIECES,)), dma((9,))],
         compiler_params=pltpu.CompilerParams(
-            collective_id=0, has_side_effects=True, vmem_limit_bytes=56 * 1024 * 1024
+            collective_id=0, has_side_effects=True, vmem_limit_bytes=40 * 1024 * 1024
         ),
     )(
-        eigenvectors,
-        jnp.swapaxes(aligned_vectors, 1, 2),
-        jnp.swapaxes(straddle_vectors, 1, 2),
+        pltpu.with_memory_space_constraint(eigenvectors, pltpu.HBM),
+        pltpu.with_memory_space_constraint(jnp.swapaxes(aligned_vectors, 1, 2), pltpu.HBM),
+        pltpu.with_memory_space_constraint(jnp.swapaxes(straddle_vectors, 1, 2), pltpu.HBM),
     )
 
 

time: 74.7 us -> 72.6 us (0.972)
  Pallas kernels: 72.9 us -> 71.8 us
  local copies, waits for them, and re-layouts: 1.67 us -> 0.71 us
    pallas_call x1, Pallas kernels: 72.9 us -> 71.8 us  [on_device(): pl.pallas_call(kernel, out_shape=jax.ShapeDtypeStruct(eigenvectors.shape,...]
    unnamed x1, local copies, waits for them, and re-layouts: 1.67 us -> 0.71 us
where the time goes in v3:
time: 72.6 us; the launch traced here: 72.5 us
  Pallas kernels  71.8 us (99%)
    pallas_call x1, Pallas kernels, on_device(): pl.pallas_call(kernel, out_shape=jax.ShapeDtypeStruct(eigenvectors.shape,...  71.8 us

profile of v3, /device:TPU:1, one launch (start us, length us, event | category | flops | bytes accessed | tf_op | source)
XLA Modules:
  0.0 72.5 jit_solution(13124891960493532929)
XLA Ops:
  0.0 71.8 %shard_map.37 = f32[512,128]{1,0:T(8,128)S(1)} custom-call(f32[512,128]{1,0:T(8,128)} %c_ref.1, f32[2,16,512]{2,1,0:T(8,128)} %bitcast.2, f32[2,16,512]{2,1,0:T(8,128)} %bitcast.3), custom_call_target="tpu_custom_call" | custom-call | tf_op jit(solution)/shard_map/pallas_call | solution.py:414
  71.8 0.7 copy.5

commit v4 on v2

--- a/solution.py
+++ b/solution.py
@@ -27,13 +27,7 @@
     )
 
 
-def lower_inverses(grams, between=()):
-    between = list(between)
-
-    def pause():
-        if between:
-            between.pop(0)()
-
+def lower_inverses(grams):
     row = lax.broadcasted_iota(jnp.int32, (NB, NB), 0)
     col = lax.broadcasted_iota(jnp.int32, (NB, NB), 1)
     on_diagonal = row == col
@@ -46,20 +40,18 @@
     for _ in range(4):
         powers = [mm(n, n) for n in powers]
         result = [t + mm(t, n) for t, n in zip(result, powers)]
-    pause()
     result = [t / d for t, d in zip(result, across)]
     for size in (32, 64, 128):
         below = (row // (2 * size) == col // (2 * size)) & (row // size > col // size)
         left = [mm(t, jnp.where(below, g, 0.0)) for t, g in zip(result, grams)]
         result = [t - mm(half, t) for t, half in zip(result, left)]
-        pause()
     return result
 
 
 def kernel(
     c_ref, a_ref, x_ref, o_ref,
-    V, C_in, Ct, gram_a, gram_l, gram_u, gram_in, t_a, t_l, t_u, g_t, h_t, b_1, b_2, m_t,
-    p_own, p_in, P_own, P_in,
+    V, C_in, Ct, gram_a, gram_l, gram_u, gram_in, t_a, t_l, t_u, g_t, b_1, b_2, m_t,
+    p_own, p_in, P_own, P_in, w_own,
     ring_send, ring_recv, row_send, row_recv, chain_send, chain_recv, local_sem,
 ):
     row = lax.axis_index("row")
@@ -102,8 +94,12 @@
         pl.semaphore_signal(barrier, inc=1, device_id=below, device_id_type=MESH)
 
     def own_block(group, half):
-        source = x_ref if group < 2 else a_ref
-        return source.at[group % 2, :, pl.ds((1 - half) * NB, NB)]
+        upper, lower = pl.ds(0, NB), pl.ds(NB, NB)
+        if group == 0:
+            return x_ref.at[half, :, upper]
+        if group == 3:
+            return x_ref.at[half, :, lower]
+        return a_ref.at[group - 1, :, upper if half == 1 else lower]
 
     def one(group, half, k):
         if half == 0:
@@ -208,16 +204,16 @@
     near_to_far(3)
 
     def x_up(s):
-        return V[s, 1].reshape(NB, NB)
+        return V[0, s].reshape(NB, NB)
 
     def x_low(s):
-        return V[s, 0].reshape(NB, NB)
+        return V[3, s].reshape(NB, NB)
 
     def a_up(s):
-        return V[2 + s, 1].reshape(NB, NB)
+        return V[1 + s, 1].reshape(NB, NB)
 
     def a_low(s):
-        return V[2 + s, 0].reshape(NB, NB)
+        return V[1 + s, 0].reshape(NB, NB)
 
     def triangle(source, target, s, base, device):
         return [
@@ -244,6 +240,7 @@
         for s in range(2)
     ]
 
+
     def upper_gram(s):
         gram_u[s] = mmt(x_up(s), x_up(s))
 
@@ -252,53 +249,50 @@
             for copy in gram_up[s]:
                 copy.start()
 
-    def aligned_products(s):
-        gram_a[s] = mmt(a_up(s), a_up(s)) + mmt(a_low(s), a_low(s))
-
-    def cross_products(s):
-        g_t[s] = mmt(x_low(s), a_low(s))
-        h_t[s] = mmt(a_up(s), x_up(s))
-
     far_finish(0)
-    upper_gram(0)
+    for s in range(2):
+        upper_gram(s)
+    far_pass(2)
     far_finish(1)
-    upper_gram(1)
-    for s in range(2):
-        gram_l[s] = mmt(x_low(s), x_low(s))
-    p_own[0] = mmt(Ct[:, NB:], x_low(0))
-
-    @pl.when(has_below)
-    def _():
-        p_down[0].start()
-
-    far_pass(2)
+    gram_a[0] = mmt(a_up(0), a_up(0)) + mmt(a_low(0), a_low(0))
     far_pass(3)
     far_finish(2)
-    aligned_products(0)
-    t_a[0] = lower_inverses([gram_a[0]])[0]
-    cross_products(0)
-    b_2[0] = mm(t_a[0], h_t[0])
+    gram_a[1] = mmt(a_up(1), a_up(1)) + mmt(a_low(1), a_low(1))
+    pair = lower_inverses([gram_a[0], gram_a[1]])
+    for s in range(2):
+        t_a[s] = pair[s]
+        b_2[s] = mm(t_a[s], mmt(a_up(s), x_up(s)))
+
+    def local_part(s):
+        upper, lower = Ct[:, :NB], Ct[:, NB:]
+        w_own[...] = mmt(upper, a_up(s)) + mmt(lower, a_low(s))
+        P_own[s] = mmt(upper, x_up(s)) - mm(w_own[...], b_2[s])
+
+    local_part(0)
     far_finish(3)
-    aligned_products(1)
-    cross_products(1)
+    gram_l[0] = mmt(x_low(0), x_low(0))
+
+    gram_l[1] = mmt(x_low(1), x_low(1))
+    p_own[0] = mmt(Ct[:, NB:], x_low(0))
 
     @pl.when(has_below)
     def _():
+        p_down[0].start()
         for s in range(2):
             for copy in gram_up[s]:
                 copy.wait_recv()
 
-    three = lower_inverses([gram_l[0] + gram_in[0], gram_l[1] + gram_in[1], gram_a[1]])
-    for s in range(2):
-        t_l[s] = three[s]
-
-        @pl.when(has_below)
-        def _():
-            for copy in t_down[s]:
-                copy.start()
-
-    t_a[1] = three[2]
-    b_2[1] = mm(t_a[1], h_t[1])
+    for s in range(2):
+        g_t[s] = mmt(x_low(s), a_low(s))
+    pair = lower_inverses([gram_l[0] + gram_in[0], gram_l[1] + gram_in[1]])
+    for s in range(2):
+        t_l[s] = pair[s]
+
+    @pl.when(has_below)
+    def _():
+        for copy in t_down[0] + t_down[1]:
+            copy.start()
+
     for s in range(2):
         b_1[s] = mm(t_l[s], g_t[s])
         m_t[s] = mm(b_1[s], b_2[s])
@@ -309,10 +303,8 @@
         for s in range(2):
             t_u[s] = own[s]
 
-    for s in range(2):
-        upper, lower = Ct[:, :NB], Ct[:, NB:]
-        w = mmt(upper, a_up(s)) + mmt(lower, a_low(s))
-        P_own[s] = mmt(upper, x_up(s)) - mm(w, b_2[s]) + mm(p_own[s], m_t[s])
+    P_own[0] += mm(p_own[0], m_t[0])
+    for s in range(2):
         for k in range(PIECES):
             piece = pl.ds(k * PIECE, PIECE)
 
@@ -325,25 +317,37 @@
             def _():
                 P_up[s][k].start()
 
+        if s == 0:
+
+            @pl.when(has_above)
+            def _():
+                for copy in t_down[0] + [p_down[0]]:
+                    copy.wait_recv()
+
         both = p_own[s] + P_in[s]
-        coeffs_a = mm(w - mm(both, b_1[s]), t_a[s])
+        coeffs_a = mm(w_own[...] - mm(both, b_1[s]), t_a[s])
         coeffs_l = mm(both, t_l[s])
-        Ct[:, NB:] = lower - mm(coeffs_l, x_low(s)) - mm(coeffs_a, a_low(s))
+        upper, lower = Ct[:, :NB], Ct[:, NB:]
+        lower = lower - mm(coeffs_l, x_low(s)) - mm(coeffs_a, a_low(s))
+        upper = upper - mm(coeffs_a, a_up(s))
+        if s == 1:
+
+            @pl.when(has_above)
+            def _():
+                for copy in t_down[1] + [p_down[1]]:
+                    copy.wait_recv()
+
+        upper = upper - mm(mm(p_in[s] + P_own[s], t_u[s]), x_up(s))
+        Ct[:, NB:] = lower
+        Ct[:, :NB] = upper
         if s == 0:
-            p_own[1] = mmt(Ct[:, NB:], x_low(1))
+            p_own[1] = mmt(lower, x_low(1))
+            local_part(1)
+            P_own[1] += mm(p_own[1], m_t[1])
 
             @pl.when(has_below)
             def _():
                 p_down[1].start()
-
-        @pl.when(has_above)
-        def _():
-            p_down[s].wait_recv()
-            for copy in t_down[s]:
-                copy.wait_recv()
-
-        coeffs_u = mm(p_in[s] + P_own[s], t_u[s])
-        Ct[:, :NB] = upper - mm(coeffs_a, a_up(s)) - mm(coeffs_u, x_up(s))
 
     o_ref[...] = Ct[...].T
 
@@ -365,7 +369,7 @@
 
 def on_device(eigenvectors, aligned_vectors, straddle_vectors):
     columns = eigenvectors.shape[1]
-    in_place = pl.BlockSpec(memory_space=pl.ANY)
+    in_place = pl.BlockSpec(memory_space=pltpu.HBM)
     square = pltpu.VMEM((2, NB, NB), jnp.float32)
     product = pltpu.VMEM((2, columns, NB), jnp.float32)
     dma = pltpu.SemaphoreType.DMA
@@ -379,16 +383,17 @@
             pltpu.VMEM(eigenvectors.shape, jnp.float32),
             pltpu.VMEM((columns, SPAN), jnp.float32),
         ]
-        + [square] * 12
+        + [square] * 11
         + [product] * 4
+        + [pltpu.VMEM((columns, NB), jnp.float32)]
         + [dma((64,)), dma((64,)), dma((10,)), dma((10,)), dma((2 * PIECES,)), dma((2 * PIECES,)), dma((9,))],
         compiler_params=pltpu.CompilerParams(
-            collective_id=0, has_side_effects=True, vmem_limit_bytes=56 * 1024 * 1024
+            collective_id=0, has_side_effects=True, vmem_limit_bytes=40 * 1024 * 1024
         ),
     )(
-        eigenvectors,
-        jnp.swapaxes(aligned_vectors, 1, 2),
-        jnp.swapaxes(straddle_vectors, 1, 2),
+        pltpu.with_memory_space_constraint(eigenvectors, pltpu.HBM),
+        pltpu.with_memory_space_constraint(jnp.swapaxes(aligned_vectors, 1, 2), pltpu.HBM),
+        pltpu.with_memory_space_constraint(jnp.swapaxes(straddle_vectors, 1, 2), pltpu.HBM),
     )
 
 

time: 74.7 us -> 71.4 us (0.956)
  Pallas kernels: 72.9 us -> 70.6 us
  local copies, waits for them, and re-layouts: 1.67 us -> 0.71 us
    pallas_call x1, Pallas kernels: 72.9 us -> 70.6 us  [on_device(): pl.pallas_call(kernel, out_shape=jax.ShapeDtypeStruct(eigenvectors.shape,...]
    unnamed x1, local copies, waits for them, and re-layouts: 1.67 us -> 0.71 us
where the time goes in v4:
time: 71.4 us; the launch traced here: 71.3 us
  Pallas kernels  70.6 us (99%)
    pallas_call x1, Pallas kernels, on_device(): pl.pallas_call(kernel, out_shape=jax.ShapeDtypeStruct(eigenvectors.shape,...  70.6 us

profile of v4, /device:TPU:1, one launch (start us, length us, event | category | flops | bytes accessed | tf_op | source)
XLA Modules:
  0.0 71.3 jit_solution(7026302469811881545)
XLA Ops:
  0.0 70.6 %shard_map.37 = f32[512,128]{1,0:T(8,128)S(1)} custom-call(f32[512,128]{1,0:T(8,128)} %c_ref.1, f32[2,16,512]{2,1,0:T(8,128)} %bitcast.2, f32[2,16,512]{2,1,0:T(8,128)} %bitcast.3), custom_call_target="tpu_custom_call" | custom-call | tf_op jit(solution)/shard_map/pallas_call | solution.py:376
  70.6 0.7 copy.5

commit v5 on v4

--- a/solution.py
+++ b/solution.py
@@ -11,6 +11,7 @@
 SIDE = 4
 PIECES = 4
 PIECE = 32
+GROUP = 4
 MESH = pl.DeviceIdType.MESH
 HIGH = lax.Precision.HIGH
 
@@ -51,8 +52,8 @@
 def kernel(
     c_ref, a_ref, x_ref, o_ref,
     V, C_in, Ct, gram_a, gram_l, gram_u, gram_in, t_a, t_l, t_u, g_t, b_1, b_2, m_t,
-    p_own, p_in, P_own, P_in, w_own,
-    ring_send, ring_recv, row_send, row_recv, chain_send, chain_recv, local_sem,
+    n_own, n_in, p_own, p_in, P_own, q_own, q_in, Z, w_own, total,
+    ring_send, ring_recv, row_send, row_recv, chain_send, chain_recv, jump_send, jump_recv, local_sem,
 ):
     row = lax.axis_index("row")
     col = lax.axis_index("col")
@@ -67,6 +68,18 @@
 
     above = ((row + last) % (last + 1), col)
     below = ((row + 1) % (last + 1), col)
+    rank, group_at = row % GROUP, row // GROUP
+    groups = (last + 1) // GROUP
+    is_top, is_bottom = rank == GROUP - 1, rank == 0
+    has_source = group_at < groups - 1
+    source = ((group_at * GROUP + GROUP) % (last + 1), col)
+
+    partner = (row + 1 - 2 * (row % 2), col)
+    hands_on = has_source & (is_top | is_bottom)
+
+    def up(distance):
+        return ((row + last + 1 - distance) % (last + 1), col)
+
     has_above = row > 0
     has_below = row < last
 
@@ -92,6 +105,16 @@
     @pl.when(has_below)
     def _():
         pl.semaphore_signal(barrier, inc=1, device_id=below, device_id_type=MESH)
+
+    sends_jump = is_bottom & has_above
+
+    @pl.when(sends_jump)
+    def _():
+        pl.semaphore_signal(barrier, inc=1, device_id=up(GROUP), device_id_type=MESH)
+
+    @pl.when(has_source & is_bottom)
+    def _():
+        pl.semaphore_signal(barrier, inc=1, device_id=source, device_id_type=MESH)
 
     def own_block(group, half):
         upper, lower = pl.ds(0, NB), pl.ds(NB, NB)
@@ -171,7 +194,9 @@
             finish(far[g, h])
 
     ends = (row + last) // (last + 1) + (2 * last - row) // (last + 1)
-    pl.semaphore_wait(barrier, 6 + ends)
+    from_lower = ((GROUP - 1 - rank) // (GROUP - 1)) * ((group_at + groups - 1) // groups)
+    from_upper = ((GROUP - 1 - rank) // (GROUP - 1)) * ((2 * (groups - 1) - group_at) // groups)
+    pl.semaphore_wait(barrier, 6 + ends + from_lower + from_upper)
     for g in range(4):
         for h in range(2):
             for copy in near[g, h]:
@@ -186,7 +211,10 @@
         for s in range(2):
             gram_in[s, HALF:] = jnp.zeros((HALF, NB), jnp.float32)
             gram_in[s, :HALF, :HALF] = jnp.zeros((HALF, HALF), jnp.float32)
-        P_in[...] = jnp.zeros_like(P_in)
+
+    @pl.when(group_at == groups - 1)
+    def _():
+        Z[...] = jnp.zeros_like(Z)
 
     @pl.when(row == 0)
     def _():
@@ -229,17 +257,47 @@
     gram_up = [triangle(gram_u, gram_in, s, 2 * s, above) for s in range(2)]
     t_down = [triangle(t_l, t_u, s, 4 + 2 * s, below) for s in range(2)]
     p_down = [remote(p_own.at[s], p_in.at[s], rows, 8 + s, below) for s in range(2)]
-    P_up = [
+    pieces = [pl.ds(k * PIECE, PIECE) for k in range(PIECES)]
+    q_up = [
         [
-            remote(
-                P_own.at[s, pl.ds(k * PIECE, PIECE)], P_in.at[s, pl.ds(k * PIECE, PIECE)],
-                chain, s * PIECES + k, above,
-            )
-            for k in range(PIECES)
+            remote(q_own.at[s, piece], q_in.at[s, piece], chain, s * PIECES + k, above)
+            for k, piece in enumerate(pieces)
         ]
         for s in range(2)
     ]
-
+    n_up = [remote(n_own.at[s], n_in.at[s], rows, 10 + s, above) for s in range(2)]
+
+    def jump(s, k, distance):
+        return pltpu.make_async_remote_copy(
+            src_ref=P_own.at[s, pieces[k]], dst_ref=Z.at[s, pieces[k]],
+            send_sem=jump_send.at[(s * PIECES + k) * GROUP + distance - 1],
+            recv_sem=jump_recv.at[s * PIECES + k],
+            device_id=up(distance), device_id_type=MESH,
+        )
+
+    def hand_on(s, k):
+        return pltpu.make_async_remote_copy(
+            src_ref=Z.at[s, pieces[k]], dst_ref=Z.at[s, pieces[k]],
+            send_sem=jump_send.at[(s * PIECES + k) * GROUP + 1],
+            recv_sem=jump_recv.at[s * PIECES + k],
+            device_id=partner, device_id_type=MESH,
+        )
+
+    def compose_top(s):
+        @pl.when(has_source & is_top)
+        def _():
+            n_own[s] = m_t[s]
+            n_up[s].start()
+
+    def compose_rest(s, takes):
+        @pl.when(has_source & takes)
+        def _():
+            n_up[s].wait_recv()
+            n_own[s] = mm(n_in[s], m_t[s])
+
+        @pl.when(has_source & takes & (rank > 0))
+        def _():
+            n_up[s].start()
 
     def upper_gram(s):
         gram_u[s] = mmt(x_up(s), x_up(s))
@@ -266,7 +324,7 @@
     def local_part(s):
         upper, lower = Ct[:, :NB], Ct[:, NB:]
         w_own[...] = mmt(upper, a_up(s)) + mmt(lower, a_low(s))
-        P_own[s] = mmt(upper, x_up(s)) - mm(w_own[...], b_2[s])
+        q_own[s] = mmt(upper, x_up(s)) - mm(w_own[...], b_2[s])
 
     local_part(0)
     far_finish(3)
@@ -303,19 +361,83 @@
         for s in range(2):
             t_u[s] = own[s]
 
-    P_own[0] += mm(p_own[0], m_t[0])
-    for s in range(2):
-        for k in range(PIECES):
-            piece = pl.ds(k * PIECE, PIECE)
-
-            @pl.when(has_below)
-            def _():
-                P_up[s][k].wait_recv()
-                P_own[s, piece] += mm(P_in[s, piece], m_t[s])
-
-            @pl.when(has_above)
-            def _():
-                P_up[s][k].start()
+    def receive(s, k, takes, hands):
+        @pl.when(takes)
+        def _():
+            jump(s, k, GROUP).wait_recv()
+
+        @pl.when(hands)
+        def _():
+            hand_on(s, k).start()
+
+    q_own[0] += mm(p_own[0], m_t[0])
+    for s in range(2):
+        if s == 1:
+            for k in range(PIECES):
+                receive(s, k, has_source & is_bottom, has_source & is_bottom)
+        for k, piece in enumerate(pieces):
+
+            @pl.when(rank < GROUP - 1)
+            def _():
+                q_up[s][k].wait_recv()
+                q_own[s, piece] += mm(q_in[s, piece], m_t[s])
+
+            @pl.when(rank > 0)
+            def _():
+                q_up[s][k].start()
+
+        if s == 0:
+            compose_top(0)
+            compose_top(1)
+            compose_rest(0, rank < GROUP - 1)
+            compose_rest(1, (rank < GROUP - 1) & (rank > 0))
+        else:
+            compose_rest(1, is_bottom)
+
+        for k, piece in enumerate(pieces):
+
+            if s == 0:
+                receive(s, k, has_source, hands_on)
+            else:
+                receive(s, k, has_source & (rank > 0), has_source & is_top)
+
+            @pl.when(has_source)
+            def _():
+                P_own[s, piece] = q_own[s, piece] + mm(Z[s, piece], n_own[s])
+
+            @pl.when(group_at == groups - 1)
+            def _():
+                P_own[s, piece] = q_own[s, piece]
+
+            @pl.when(sends_jump & (group_at > 1))
+            def _():
+                jump(s, k, GROUP).start()
+
+            @pl.when(sends_jump & (group_at == 1))
+            def _():
+                jump(s, k, 1).start()
+
+        @pl.when(sends_jump & (group_at > 1))
+        def _():
+            for k in range(PIECES):
+                jump(s, k, 1).start()
+
+        @pl.when(sends_jump & (group_at == 1))
+        def _():
+            for k in range(PIECES):
+                jump(s, k, GROUP).start()
+
+        @pl.when(is_top)
+        def _():
+            total[...] = p_own[s] + Z[s]
+
+        @pl.when((rank < GROUP - 1) & has_source)
+        def _():
+            total[...] = p_own[s] + q_in[s] + mm(Z[s], n_in[s])
+
+        @pl.when((rank < GROUP - 1) & (group_at == groups - 1))
+        def _():
+            total[...] = p_own[s] + q_in[s]
 
         if s == 0:
 
@@ -324,7 +446,7 @@
                 for copy in t_down[0] + [p_down[0]]:
                     copy.wait_recv()
 
-        both = p_own[s] + P_in[s]
+        both = total[...]
         coeffs_a = mm(w_own[...] - mm(both, b_1[s]), t_a[s])
         coeffs_l = mm(both, t_l[s])
         upper, lower = Ct[:, :NB], Ct[:, NB:]
@@ -343,7 +465,7 @@
         if s == 0:
             p_own[1] = mmt(lower, x_low(1))
             local_part(1)
-            P_own[1] += mm(p_own[1], m_t[1])
+            q_own[1] += mm(p_own[1], m_t[1])
 
             @pl.when(has_below)
             def _():
@@ -358,8 +480,31 @@
 
     @pl.when(has_above)
     def _():
-        for copy in gram_up[0] + gram_up[1] + P_up[0] + P_up[1]:
+        for copy in gram_up[0] + gram_up[1]:
             copy.wait_send()
+
+    @pl.when(rank > 0)
+    def _():
+        for copy in q_up[0] + q_up[1]:
+            copy.wait_send()
+
+    @pl.when(has_source & (rank > 0))
+    def _():
+        for copy in n_up:
+            copy.wait_send()
+
+    @pl.when(sends_jump)
+    def _():
+        for s in range(2):
+            for k in range(PIECES):
+                jump(s, k, 1).wait_send()
+                jump(s, k, GROUP).wait_send()
+
+    @pl.when(hands_on)
+    def _():
+        for s in range(2):
+            for k in range(PIECES):
+                hand_on(s, k).wait_send()
 
     @pl.when(has_below)
     def _():
@@ -383,10 +528,12 @@
             pltpu.VMEM(eigenvectors.shape, jnp.float32),
             pltpu.VMEM((columns, SPAN), jnp.float32),
         ]
-        + [square] * 11
-        + [product] * 4
-        + [pltpu.VMEM((columns, NB), jnp.float32)]
-        + [dma((64,)), dma((64,)), dma((10,)), dma((10,)), dma((2 * PIECES,)), dma((2 * PIECES,)), dma((9,))],
+        + [square] * 13
+        + [product] * 6
+        + [pltpu.VMEM((columns, NB), jnp.float32)] * 2
+        + [dma((64,)), dma((64,)), dma((12,)), dma((12,))]
+        + [dma((2 * PIECES,)), dma((2 * PIECES,))]
+        + [dma((2 * PIECES * GROUP,)), dma((2 * PIECES,)), dma((9,))],
         compiler_params=pltpu.CompilerParams(
             collective_id=0, has_side_effects=True, vmem_limit_bytes=40 * 1024 * 1024
         ),

time: 71.4 us -> 73.4 us (1.028)
  Pallas kernels: 70.6 us -> 72.6 us
    pallas_call x1, Pallas kernels: 70.6 us -> 72.6 us  [on_device(): pl.pallas_call(kernel, out_shape=jax.ShapeDtypeStruct(eigenvectors.shape,...]
where the time goes in v5:
time: 73.4 us; the launch traced here: 73.3 us
  Pallas kernels  72.6 us (99%)
    pallas_call x1, Pallas kernels, on_device(): pl.pallas_call(kernel, out_shape=jax.ShapeDtypeStruct(eigenvectors.shape,...  72.6 us

profile of v5, /device:TPU:1, one launch (start us, length us, event | category | flops | bytes accessed | tf_op | source)
XLA Modules:
  0.0 73.3 jit_solution(15246838541327430534)
XLA Ops:
  0.0 72.6 %shard_map.37 = f32[512,128]{1,0:T(8,128)S(1)} custom-call(f32[512,128]{1,0:T(8,128)} %c_ref.1, f32[2,16,512]{2,1,0:T(8,128)} %bitcast.2, f32[2,16,512]{2,1,0:T(8,128)} %bitcast.3), custom_call_target="tpu_custom_call" | custom-call | tf_op jit(solution)/shard_map/pallas_call | solution.py:521
  72.6 0.7 copy.5

commit v6 on v4

--- a/solution.py
+++ b/solution.py
@@ -9,8 +9,8 @@
 SPAN = 2 * NB
 HALF = NB // 2
 SIDE = 4
-PIECES = 4
-PIECE = 32
+PIECES = 8
+PIECE = 128 // PIECES
 MESH = pl.DeviceIdType.MESH
 HIGH = lax.Precision.HIGH
 
@@ -229,17 +229,9 @@
     gram_up = [triangle(gram_u, gram_in, s, 2 * s, above) for s in range(2)]
     t_down = [triangle(t_l, t_u, s, 4 + 2 * s, below) for s in range(2)]
     p_down = [remote(p_own.at[s], p_in.at[s], rows, 8 + s, below) for s in range(2)]
-    P_up = [
-        [
-            remote(
-                P_own.at[s, pl.ds(k * PIECE, PIECE)], P_in.at[s, pl.ds(k * PIECE, PIECE)],
-                chain, s * PIECES + k, above,
-            )
-            for k in range(PIECES)
-        ]
-        for s in range(2)
-    ]
-
+    def P_up(s, k):
+        piece = pl.ds(pl.multiple_of(k * PIECE, PIECE), PIECE)
+        return remote(P_own.at[s, piece], P_in.at[s, piece], chain, s * PIECES + k, above)
 
     def upper_gram(s):
         gram_u[s] = mmt(x_up(s), x_up(s))
@@ -303,19 +295,31 @@
         for s in range(2):
             t_u[s] = own[s]
 
+    def drain():
+        for stages in (near, far):
+            for stage in stages.values():
+                for copy in stage:
+                    copy.wait_send()
+
     P_own[0] += mm(p_own[0], m_t[0])
-    for s in range(2):
-        for k in range(PIECES):
-            piece = pl.ds(k * PIECE, PIECE)
+
+    @pl.when(row < last - 1)
+    def _():
+        drain()
+
+    for s in range(2):
+        @pl.loop(0, PIECES)
+        def _(k):
+            piece = pl.ds(pl.multiple_of(k * PIECE, PIECE), PIECE)
 
             @pl.when(has_below)
             def _():
-                P_up[s][k].wait_recv()
+                P_up(s, k).wait_recv()
                 P_own[s, piece] += mm(P_in[s, piece], m_t[s])
 
             @pl.when(has_above)
             def _():
-                P_up[s][k].start()
+                P_up(s, k).start()
 
         if s == 0:
 
@@ -351,15 +355,19 @@
 
     o_ref[...] = Ct[...].T
 
-    for stages in (near, far):
-        for stage in stages.values():
-            for copy in stage:
-                copy.wait_send()
+    @pl.when(row >= last - 1)
+    def _():
+        drain()
 
     @pl.when(has_above)
     def _():
-        for copy in gram_up[0] + gram_up[1] + P_up[0] + P_up[1]:
+        for copy in gram_up[0] + gram_up[1]:
             copy.wait_send()
+
+        @pl.loop(0, PIECES)
+        def _(k):
+            for s in range(2):
+                P_up(s, k).wait_send()
 
     @pl.when(has_below)
     def _():

time: 71.4 us -> 70.3 us (0.985)
  Pallas kernels: 70.6 us -> 69.5 us
    pallas_call x1, Pallas kernels: 70.6 us -> 69.5 us  [on_device(): pl.pallas_call(kernel, out_shape=jax.ShapeDtypeStruct(eigenvectors.shape,...]
where the time goes in v6:
time: 70.3 us; the launch traced here: 70.2 us
  Pallas kernels  69.5 us (99%)
  local copies, waits for them, and re-layouts  0.71 us (1%)
    pallas_call x1, Pallas kernels, on_device(): pl.pallas_call(kernel, out_shape=jax.ShapeDtypeStruct(eigenvectors.shape,...  69.5 us

profile of v6, /device:TPU:1, one launch (start us, length us, event | category | flops | bytes accessed | tf_op | source)
XLA Modules:
  0.0 70.2 jit_solution(15473668766357016232)
XLA Ops:
  0.0 69.5 %shard_map.37 = f32[512,128]{1,0:T(8,128)S(1)} custom-call(f32[512,128]{1,0:T(8,128)} %c_ref.1, f32[2,16,512]{2,1,0:T(8,128)} %bitcast.2, f32[2,16,512]{2,1,0:T(8,128)} %bitcast.3), custom_call_target="tpu_custom_call" | custom-call | tf_op jit(solution)/shard_map/pallas_call | solution.py:384
  69.5 0.7 %copy.5 = f32[512,128]{1,0:T(8,128)} copy(f32[512,128]{1,0:T(8,128)S(1)} %shard_map.37) | data formatting | bytes 524288

commit v7 on v6

--- a/solution.py
+++ b/solution.py
@@ -149,7 +149,7 @@
             base = 8 * (2 * g + h)
             axes = (at_x, at_y) if h == 0 else (at_y, at_x)
             near[g, h] = [
-                remote(own_block(g, h), one(g, h, 0), ring, base + i, axes[0](k))
+                remote(one(g, h, 0), one(g, h, 0), ring, base + i, axes[0](k))
                 for i, k in enumerate((1, -1, 2))
             ]
             far[g, h] = ring_stage(
@@ -170,6 +170,8 @@
         for h in range(2):
             finish(far[g, h])
 
+    for copy in own_copies:
+        copy.wait()
     ends = (row + last) // (last + 1) + (2 * last - row) // (last + 1)
     pl.semaphore_wait(barrier, 6 + ends)
     for g in range(4):
@@ -192,8 +194,6 @@
     def _():
         p_in[...] = jnp.zeros_like(p_in)
 
-    for copy in own_copies:
-        copy.wait()
     near_to_far(0)
     near_to_far(1)
     c_copy.wait()

time: 70.3 us -> 70.1 us (level)
  no operation moved by 1% of the time
where the time goes in v7:
time: 70.1 us; the launch traced here: 70 us
  Pallas kernels  69.3 us (99%)
  local copies, waits for them, and re-layouts  0.71 us (1%)
    pallas_call x1, Pallas kernels, on_device(): pl.pallas_call(kernel, out_shape=jax.ShapeDtypeStruct(eigenvectors.shape,...  69.3 us

profile of v7, /device:TPU:1, one launch (start us, length us, event | category | flops | bytes accessed | tf_op | source)
XLA Modules:
  0.0 70.0 jit_solution(5667171027279680750)
XLA Ops:
  0.0 69.3 %shard_map.37 = f32[512,128]{1,0:T(8,128)S(1)} custom-call(f32[512,128]{1,0:T(8,128)} %c_ref.1, f32[2,16,512]{2,1,0:T(8,128)} %bitcast.2, f32[2,16,512]{2,1,0:T(8,128)} %bitcast.3), custom_call_target="tpu_custom_call" | custom-call | tf_op jit(solution)/shard_map/pallas_call | solution.py:384
  69.3 0.7 %copy.5 = f32[512,128]{1,0:T(8,128)} copy(f32[512,128]{1,0:T(8,128)S(1)} %shard_map.37) | data formatting | bytes 524288

commit v8 on v7

--- a/solution.py
+++ b/solution.py
@@ -81,18 +81,6 @@
     rows = (row_send, row_recv)
     chain = (chain_send, chain_recv)
 
-    barrier = pltpu.get_barrier_semaphore()
-    for device in (at_x(1), at_x(2), at_x(3), at_y(1), at_y(2), at_y(3)):
-        pl.semaphore_signal(barrier, inc=1, device_id=device, device_id_type=MESH)
-
-    @pl.when(has_above)
-    def _():
-        pl.semaphore_signal(barrier, inc=1, device_id=above, device_id_type=MESH)
-
-    @pl.when(has_below)
-    def _():
-        pl.semaphore_signal(barrier, inc=1, device_id=below, device_id_type=MESH)
-
     def own_block(group, half):
         upper, lower = pl.ds(0, NB), pl.ds(NB, NB)
         if group == 0:
@@ -119,6 +107,18 @@
     for copy in own_copies:
         copy.start()
     c_copy.start()
+
+    barrier = pltpu.get_barrier_semaphore()
+    for device in (at_x(1), at_x(2), at_x(3), at_y(1), at_y(2), at_y(3)):
+        pl.semaphore_signal(barrier, inc=1, device_id=device, device_id_type=MESH)
+
+    @pl.when(has_above)
+    def _():
+        pl.semaphore_signal(barrier, inc=1, device_id=above, device_id_type=MESH)
+
+    @pl.when(has_below)
+    def _():
+        pl.semaphore_signal(barrier, inc=1, device_id=below, device_id_type=MESH)
 
     def ring_stage(base, own, slot, device, split):
         first, second = pl.ds(0, split), pl.ds(split, split)

time: 70.1 us -> 70.1 us (level)
  no operation moved by 1% of the time
where the time goes in v8:
time: 70.1 us
  Pallas kernels  69.3 us (99%)
  local copies, waits for them, and re-layouts  0.71 us (1%)
    pallas_call x1, Pallas kernels, on_device(): pl.pallas_call(kernel, out_shape=jax.ShapeDtypeStruct(eigenvectors.shape,...  69.3 us

profile of v8, /device:TPU:1, one launch (start us, length us, event | category | flops | bytes accessed | tf_op | source)
XLA Modules:
  0.0 70.1 jit_solution(9975976547421292750)
XLA Ops:
  0.0 69.3 %shard_map.37 = f32[512,128]{1,0:T(8,128)S(1)} custom-call(f32[512,128]{1,0:T(8,128)} %c_ref.1, f32[2,16,512]{2,1,0:T(8,128)} %bitcast.2, f32[2,16,512]{2,1,0:T(8,128)} %bitcast.3), custom_call_target="tpu_custom_call" | custom-call | tf_op jit(solution)/shard_map/pallas_call | solution.py:384
  69.4 0.7 %copy.5 = f32[512,128]{1,0:T(8,128)} copy(f32[512,128]{1,0:T(8,128)S(1)} %shard_map.37) | data formatting | bytes 524288
